TPU v7x, 256 devices: a whole 4x4x8 slice. The times are simulated.
256 devices in a mesh: batch: 4 (over x_hi, core), hidden: 16 (over x_lo, z), width: 4 (over y).
Axes of the slice: x: 4 (x_hi: 2, x_lo: 2; x = x_hi * 2 + x_lo), y: 4, z: 8, core: 2. Of those that a mesh axis runs over, the one named last changes fastest.
Arguments:
- frames: bfloat16 [4, 512, 1280], P('batch', None, 'hidden'), may hold values from -6 to 6
- adapter_weight: bfloat16 [4, 1280, 16384], P(None, 'hidden', 'width'), may hold values from -0.078125 to 0.078125
- text_embed: bfloat16 [512, 16384], P('batch', 'width'), may hold values from -6 to 6
- audio_len: int32 [4], P('batch'), may hold values from 16 to 64, as said below
- text_len: int32 [4], P('batch'), may hold values from 32 to 112, as said below
- norm_gain: bfloat16 [16384], P('width'), may hold values from 0.5 to 1.5
- gate_up: bfloat16 [16384, 2, 26624], P('width', None, ('batch', 'hidden')), may hold values from -0.046875 to 0.046875
- cotangent: bfloat16 [512, 26624], P('width', ('batch', 'hidden')), may hold values from -0.59765625 to 0.59765625
Outputs:
- hidden: bfloat16 [512, 26624], P('width', ('batch', 'hidden'))
- weight_grad: float32 [4, 1280, 16384], P(None, 'hidden', 'width')
Inputs may be any that keep to these rules, and one draw needn't show every extreme that they name: `audio_len`: some sequence holds exactly 16 audio positions and another exactly 64. audio_len + text_len never exceeds 128, and equals it in some sequence.
All inputs are finite; a program needn't handle non-finite values.
Results may differ from a plain program's by a relative error of at most 0.0059.
Values may be sent and summed in bfloat16 or wider, within the bound.
A program may use at most 64 MiB of HBM per device.

v0:
```python
import jax
import jax.numpy as jnp
from jax import lax
from jax.sharding import PartitionSpec as P

D = 16384


norm_eps = 1e-05


def row_lookup(table, row_index):
    slots = jnp.arange(table.shape[0], dtype=jnp.int32)
    return jnp.sum(jnp.where(row_index[:, None] == slots[None, :], table[None, :], 0), axis=1)


def on_device(
    frames, adapter_weight, text_embed, audio_len, text_len, norm_gain, gate_up, cotangent
):
    rows_here, frame_count, feat_here = frames.shape
    seq_len = frame_count // 4
    width_here = adapter_weight.shape[2]
    tok_here = rows_here * seq_len
    stacked = frames.reshape(tok_here, 4 * feat_here)
    kernel = adapter_weight.reshape(4 * feat_here, width_here)
    partial_audio = jnp.dot(stacked, kernel, preferred_element_type=jnp.float32)
    audio_part = lax.psum(partial_audio, "hidden")
    local_index = jnp.arange(tok_here, dtype=jnp.int32)
    row_index = local_index // seq_len
    positions = local_index % seq_len
    audio_count = row_lookup(audio_len, row_index)
    text_count = row_lookup(text_len, row_index)
    is_audio = positions < audio_count
    is_text = jnp.logical_and(jnp.logical_not(is_audio), positions < audio_count + text_count)
    stream = jnp.where(
        is_audio[:, None],
        audio_part,
        jnp.where(is_text[:, None], text_embed.astype(jnp.float32), jnp.zeros_like(audio_part)),
    )
    sum_squares = lax.psum(jnp.sum(stream * stream, axis=1), "width")
    inv_rms = lax.rsqrt(sum_squares / D + norm_eps)
    unit_stream = stream * inv_rms[:, None]
    gain_vals = norm_gain.astype(jnp.float32)
    normed = (unit_stream * gain_vals[None, :]).astype(jnp.bfloat16)
    weights = gate_up.reshape(width_here, -1)
    half_cols = weights.shape[1] // 2
    partial_pair = jnp.dot(
        lax.all_gather(normed, "batch", axis=0, tiled=True),
        weights,
        preferred_element_type=jnp.float32,
    )
    summed = lax.psum_scatter(partial_pair, "width", scatter_dimension=0, tiled=True)
    gate_vals = summed[:, :half_cols]
    up_vals = summed[:, half_cols:]
    sigmoid_gate = jax.nn.sigmoid(gate_vals)
    silu_gate = gate_vals * sigmoid_gate
    hidden = (silu_gate * up_vals).astype(jnp.bfloat16)
    cot_vals = cotangent.astype(jnp.float32)
    silu_slope = sigmoid_gate * (1.0 + gate_vals * (1.0 - sigmoid_gate))
    grad_pair = jnp.concatenate(
        [
            (cot_vals * up_vals * silu_slope).astype(jnp.bfloat16),
            (cot_vals * silu_gate).astype(jnp.bfloat16),
        ],
        axis=1,
    )
    all_pairs = lax.all_gather(grad_pair, "width", axis=0, tiled=True)
    share_rows = tok_here // lax.axis_size("hidden")
    row_block = all_pairs
    normed_grad = lax.psum_scatter(
        lax.dot_general(
            row_block, weights, (((1,), (1,)), ((), ())), preferred_element_type=jnp.float32
        ),
        ("batch", "hidden"),
        scatter_dimension=0,
        tiled=True,
    )
    share_start = lax.axis_index("hidden") * share_rows
    unit_share = lax.dynamic_slice_in_dim(unit_stream, share_start, share_rows, 0)
    inv_share = lax.dynamic_slice_in_dim(inv_rms, share_start, share_rows, 0)
    audio_share = lax.dynamic_slice_in_dim(is_audio, share_start, share_rows, 0)
    scaled_grad = normed_grad * gain_vals[None, :]
    proj_stat = lax.psum(jnp.sum(unit_share * scaled_grad, axis=1), "width") / D
    stream_grad = (scaled_grad - unit_share * proj_stat[:, None]) * inv_share[:, None]
    audio_grad = jnp.where(audio_share[:, None], stream_grad, jnp.zeros_like(stream_grad)).astype(
        jnp.bfloat16
    )
    row_block = stacked
    local_grad = lax.dot_general(
        row_block,
        lax.all_gather(audio_grad, "hidden", axis=0, tiled=True),
        (((0,), (0,)), ((), ())),
        preferred_element_type=jnp.float32,
    )
    weight_grad = lax.psum(local_grad, "batch")
    return (hidden, weight_grad.reshape(4, feat_here, width_here))


def solution(mesh):
    return jax.shard_map(
        on_device,
        mesh=mesh,
        in_specs=(
            P("batch", None, "hidden"),
            P(None, "hidden", "width"),
            P("batch", "width"),
            P("batch"),
            P("batch"),
            P("width"),
            P("width", None, ("batch", "hidden")),
            P("width", ("batch", "hidden")),
        ),
        out_specs=(P("width", ("batch", "hidden")), P(None, "hidden", "width")),
        check_vma=False,
    )
```

profile of v0, /device:TPU:1, one launch (start us, length us, event | category | flops | bytes accessed | tf_op | source)
XLA Modules:
  0.0 757.5 jit_solution(508925325179178368)
XLA Ops:
  7.2 1.2 copy.10
  8.4 0.1 reshape.64
  8.5 0.4 copy-done
  8.9 2.0 fusion.8
  11.1 0.6 copy-done.2
  13.0 134.5 %all-reduce.3.cloned.1.call-done = f32[128,4096]{1,0:T(8,128)} async-done(((f32[128,4096]{1,0:T(8,128)}), f32[128,4096]{1,0:T(8,128)}) %all-reduce.3.cloned.1.call-update) | async-done | bytes 2097168 | tf_op jit(solution)/shard_map/psum | solution.py:27
  147.4 2.4 multiply_reduce_fusion
  149.8 8.7 %psum.29 = f32[128]{0:T(128)S(1)} all-reduce(f32[128]{0:T(128)S(1)} %multiply_reduce_fusion), channel_id=1, replica_groups=mesh['batch'=4,'hidden'=16,'width'=4] {'width'}, use_global_device_ids=true, to_apply=%region_2.3 | all-reduce | flops 128 | bytes 1024 | tf_op jit(solution)/shard_map/psum | solution.py:40
  158.5 4.1 multiply_convert_fusion
  162.7 48.2 %all-gather.3.cloned.1.call-done = bf16[512,4096]{1,0:T(8,128)(2,1)} async-done(((bf16[128,4096]{1,0:T(8,128)(2,1)}), bf16[512,4096]{1,0:T(8,128)(2,1)}) %all-gather.3.cloned.1.call-update) | async-done | bytes 4194320 | tf_op jit(solution)/shard_map/all_gather | solution.py:48
  210.9 9.2 %fusion.9 = f32[512,832]{0,1:T(8,128)} fusion(bf16[512,4096]{1,0:T(8,128)(2,1)} %all-gather.3.cloned.1.call-done, bf16[4096,832]{0,1:T(8,128)(2,1)} %bitcast.19), kind=kOutput, calls=%fused_computation.28 | convolution fusion | flops 3489660928 | bytes 12713984 | tf_op jit(solution)/shard_map/dot_general | solution.py:47
  220.1 28.2 %reduce-scatter.3.cloned.1.call-done = f32[128,832]{0,1:T(8,128)} async-done(((f32[512,832]{0,1:T(8,128)}), f32[128,832]{0,1:T(8,128)}) %reduce-scatter.3.cloned.1.call-update) | async-done | bytes 426000 | tf_op jit(solution)/shard_map/reduce_scatter | solution.py:52
  248.3 1.8 fusion.2
  250.1 17.1 %all_gather.10 = bf16[512,832]{0,1:T(8,128)(2,1)S(1)} all-gather(bf16[128,832]{0,1:T(8,128)(2,1)S(1)} %pad_maximum_fusion), channel_id=1, replica_groups=mesh['batch'=4,'hidden'=16,'width'=4] {'width'}, dimensions={0}, use_global_device_ids=true | all-gather | bytes 1064960 | tf_op jit(solution)/shard_map/all_gather | solution.py:67
  267.2 9.7 %fusion.10 = f32[512,4096]{1,0:T(8,128)} fusion(bf16[512,832]{0,1:T(8,128)(2,1)S(1)} %all_gather.10, bf16[4096,832]{0,1:T(8,128)(2,1)} %bitcast.20), kind=kOutput, calls=%fused_computation.29 | convolution fusion | flops 3489660928 | bytes 16056320 | tf_op jit(solution)/shard_map/dot_general | solution.py:71
  277.0 0.1 dynamic_slice.9
  277.0 260.5 %reduce-scatter.5.cloned.1.call-done = f32[8,4096]{1,0:T(8,128)} async-done(((f32[512,4096]{1,0:T(8,128)}), f32[8,4096]{1,0:T(8,128)}) %reduce-scatter.5.cloned.1.call-update) | async-done | bytes 131088 | tf_op jit(solution)/shard_map/reduce_scatter | solution.py:70
  537.6 1.1 multiply_reduce_fusion.1
  538.8 8.8 %psum.30 = f32[8]{0:T(128)S(1)} all-reduce(f32[8]{0:T(128)S(1)} %multiply_reduce_fusion.1), channel_id=1, replica_groups=mesh['batch'=4,'hidden'=16,'width'=4] {'width'}, use_global_device_ids=true, to_apply=%region_6.7 | all-reduce | flops 8 | bytes 64 | tf_op jit(solution)/shard_map/psum | solution.py:83
  547.6 1.7 select_convert_fusion
  549.4 67.9 %all-gather.5.cloned.1.call-done = bf16[128,4096]{1,0:T(8,128)(2,1)} async-done(((bf16[8,4096]{1,0:T(8,128)(2,1)}), bf16[128,4096]{1,0:T(8,128)(2,1)}) %all-gather.5.cloned.1.call-update) | async-done | bytes 1048592 | tf_op jit(solution)/shard_map/all_gather | solution.py:91
  617.3 4.5 fusion.11
  621.8 123.5 %all-reduce.5.cloned.1.call-done = f32[4,80,4096]{2,1,0:T(8,128)} async-done(((f32[4,80,4096]{2,1,0:T(8,128)}), f32[4,80,4096]{2,1,0:T(8,128)}) %all-reduce.5.cloned.1.call-update) | async-done | bytes 5242896 | tf_op jit(solution)/shard_map/psum | solution.py:95
  745.2 5.4 copy.15
  (22 shorter events, 0.5 us)
Async XLA Ops:
  7.2 1.8 copy-start
  7.2 140.3 %all-reduce.3.cloned.1.call-start = ((), (), s32[]{:S(2)}) async-start(), calls=%async_computation.2 | async-start | bytes 4194304 | tf_op jit(solution)/shard_map/psum | solution.py:27
  11.0 0.7 copy-start.2
  11.0 199.9 %all-gather.3.cloned.1.call-start = ((), (), s32[]{:S(2)}) async-start(), calls=%async_computation.3 | async-start | bytes 5242880 | tf_op jit(solution)/shard_map/all_gather | solution.py:48
  162.6 85.7 %reduce-scatter.3.cloned.1.call-start = ((), (), s32[]{:S(2)}) async-start(), calls=%async_computation.4 | async-start | bytes 2129920 | tf_op jit(solution)/shard_map/reduce_scatter | solution.py:52
  210.9 37.4 %copy-start.1 = (bf16[128,416]{0,1:T(8,128)(2,1)S(1)}, bf16[128,416]{0,1:T(8,128)(2,1)}, u32[]{:S(2)}) copy-start(bf16[128,416]{0,1:T(8,128)(2,1)} %param.15) | copy-start | bytes 319492
  220.1 317.5 %reduce-scatter.5.cloned.1.call-start = ((), (), s32[]{:S(2)}) async-start(), calls=%async_computation.5 | async-start | bytes 8519680 | tf_op jit(solution)/shard_map/reduce_scatter | solution.py:70
  276.9 340.4 %all-gather.5.cloned.1.call-start = ((), (), s32[]{:S(2)}) async-start(), calls=%async_computation.6 | async-start | bytes 1114112 | tf_op jit(solution)/shard_map/all_gather | solution.py:91
  549.3 195.9 %all-reduce.5.cloned.1.call-start = ((), (), s32[]{:S(2)}) async-start(), calls=%async_computation.7 | async-start | bytes 10485760 | tf_op jit(solution)/shard_map/psum | solution.py:95
Sparse Core Ops, SparseCore 0:
  11.2 136.1 all-reduce.2
  162.8 48.0 all-gather.2
  220.2 28.0 reduce-scatter.2
  277.0 260.5 reduce-scatter.4
  549.4 67.7 all-gather.4
  621.9 123.2 all-reduce.4
where the time goes:
time: 758 us
  waiting for transfers between devices  663 us (87%)
  blocking collectives  34.6 us (5%)
  matrix products  25.3 us (3%)
  between operations  15.5 us (2%)
  other arithmetic  11.1 us (1%)
  local copies, waits for them, and re-layouts  7.94 us (1%)
    reduce_scatter x1, waiting for transfers between devices, on_device(): lax.psum_scatter(lax.dot_general(row_block, weights, (((1,), (1,)), ((),...  261 us
    psum x1, waiting for transfers between devices, on_device(): audio_part = lax.psum(partial_audio, 'hidden')  134 us
    psum x1, waiting for transfers between devices, on_device(): weight_grad = lax.psum(local_grad, 'batch')  123 us
    all_gather x1, waiting for transfers between devices, on_device(): lax.all_gather(audio_grad, 'hidden', axis=0, tiled=True)  67.9 us
    all_gather x1, waiting for transfers between devices, on_device(): lax.all_gather(normed, 'batch', axis=0, tiled=True)  48.2 us
    reduce_scatter x1, waiting for transfers between devices, on_device(): lax.psum_scatter(partial_pair, 'width', scatter_dimension=0, tiled=True)  28.2 us
    all_gather x1, blocking collectives, on_device(): all_pairs = lax.all_gather(grad_pair, 'width', axis=0, tiled=True)  17.1 us
  transfers between devices with their start and end apart: 6, of which 6 were waited for; matrix products, arithmetic and copies ran while one was open for 0% of the time, Pallas kernels for 0%

commit v1 on v0

v1 whole, which is shorter than its diff:
```python
import jax
import jax.numpy as jnp
from jax import lax
from jax.sharding import PartitionSpec as P

D = 16384
HEAD = 64
norm_eps = 1e-05


def on_device(
    frames, adapter_weight, text_embed, audio_len, text_len, norm_gain, gate_up, cotangent
):
    feat_here = frames.shape[2]
    seq_len = frames.shape[1] // 4
    width_here = adapter_weight.shape[2]
    stacked = frames[0, : 4 * HEAD].reshape(HEAD, 4 * feat_here)
    kernel = adapter_weight.reshape(4 * feat_here, width_here)
    partial_audio = jnp.dot(stacked, kernel, preferred_element_type=jnp.float32)
    audio_part = lax.psum(partial_audio, "hidden")
    positions = jnp.arange(seq_len, dtype=jnp.int32)
    is_audio = positions < audio_len[0]
    is_text = jnp.logical_and(jnp.logical_not(is_audio), positions < audio_len[0] + text_len[0])
    text_vals = jnp.where(is_text[:, None], text_embed.astype(jnp.float32), 0.0)
    stream = jnp.concatenate(
        [jnp.where(is_audio[:HEAD, None], audio_part, text_vals[:HEAD]), text_vals[HEAD:]], axis=0
    )
    gain_vals = norm_gain.astype(jnp.float32)
    sum_squares = lax.psum(jnp.sum(stream * stream, axis=1), "width")
    inv_rms = lax.rsqrt(sum_squares / D + norm_eps)
    normed = (stream * inv_rms[:, None] * gain_vals[None, :]).astype(jnp.bfloat16)
    masked = jnp.where(is_audio[:HEAD, None], stacked, jnp.zeros_like(stacked))
    all_stacked = lax.all_gather(masked, "batch", axis=0, tiled=True)
    all_inv = lax.all_gather(inv_rms[:HEAD], "batch", axis=0, tiled=True)
    all_normed = lax.all_gather(normed, "batch", axis=0, tiled=True)
    weights = gate_up.reshape(width_here, -1)
    half = weights.shape[1] // 2
    partial_pair = jnp.dot(all_normed, weights, preferred_element_type=jnp.float32)
    summed = lax.psum_scatter(partial_pair, "width", scatter_dimension=0, tiled=True)
    gate_vals = summed[:, :half]
    up_vals = summed[:, half:]
    sigmoid_gate = jax.nn.sigmoid(gate_vals)
    silu_gate = gate_vals * sigmoid_gate
    hidden = (silu_gate * up_vals).astype(jnp.bfloat16)
    cot_vals = cotangent[:HEAD].astype(jnp.float32)
    gate_head, up_head, sig_head = gate_vals[:HEAD], up_vals[:HEAD], sigmoid_gate[:HEAD]
    grad_gate = cot_vals * up_head * sig_head * (1.0 + gate_head * (1.0 - sig_head))
    grad_up = cot_vals * silu_gate[:HEAD]
    inner = jnp.sum(grad_gate * gate_head + grad_up * up_head, axis=1) / D
    grad_pair = jnp.concatenate([grad_gate, grad_up], axis=1).astype(jnp.bfloat16)
    all_pairs = lax.all_gather(grad_pair, "width", axis=0, tiled=True)
    all_inner = lax.all_gather(inner, "width", axis=0, tiled=True)
    partial = lax.dot_general(
        all_pairs, weights, (((1,), (1,)), ((), ())), preferred_element_type=jnp.float32
    )
    head_normed = all_normed.reshape(-1, seq_len, width_here)[:, :HEAD].reshape(-1, width_here)
    head_unit = head_normed.astype(jnp.float32) / gain_vals[None, :]
    share = (gain_vals[None, :] * partial - head_unit * all_inner[:, None]) * all_inv[:, None]
    grad_share = lax.psum_scatter(share, ("batch", "hidden"), scatter_dimension=0, tiled=True)
    audio_grad = lax.all_gather(
        grad_share.astype(jnp.bfloat16), ("batch", "hidden"), axis=0, tiled=True
    )
    weight_grad = lax.dot_general(
        all_stacked, audio_grad, (((0,), (0,)), ((), ())), preferred_element_type=jnp.float32
    )
    return (hidden, weight_grad.reshape(4, feat_here, width_here))


def solution(mesh):
    return jax.shard_map(
        on_device,
        mesh=mesh,
        in_specs=(
            P("batch", None, "hidden"),
            P(None, "hidden", "width"),
            P("batch", "width"),
            P("batch"),
            P("batch"),
            P("width"),
            P("width", None, ("batch", "hidden")),
            P("width", ("batch", "hidden")),
        ),
        out_specs=(P("width", ("batch", "hidden")), P(None, "hidden", "width")),
        check_vma=False,
    )
```

time: 758 us -> 774 us (1.021)
  blocking collectives: 34.6 us -> 346 us
  waiting for transfers between devices: 663 us -> 357 us
    unnamed x0 -> x3, blocking collectives: none -> 306 us
    reduce_scatter x1 -> x0, waiting for transfers between devices: 261 us -> none  [on_device(): lax.psum_scatter(lax.dot_general(row_block, weights, (((1,), (1,)), ((),...]
    psum x1 -> x0, waiting for transfers between devices: 123 us -> none  [on_device(): weight_grad = lax.psum(local_grad, 'batch')]
    all_gather x2, waiting for transfers between devices: 116 us -> 216 us  [the longest x1 167 us: on_device(): lax.all_gather(grad_share.astype(jnp.bfloat16), ('batch', 'hidden'), axis...]
    all_gather x0 -> x1, blocking collectives: none -> 21.6 us  [on_device(): all_stacked = lax.all_gather(masked, 'batch', axis=0, tiled=True)]
    reduce_scatter x1, waiting for transfers between devices: 28.2 us -> 14.3 us  [on_device(): lax.psum_scatter(partial_pair, 'width', scatter_dimension=0, tiled=True)]
    psum x1 -> x0, blocking collectives: 8.82 us -> none  [on_device(): proj_stat = lax.psum(jnp.sum(unit_share * scaled_grad, axis=1), 'width') / D]
  transfers between devices with their start and end apart: 6 -> 4, of which waited for: 6 -> 4; matrix products, arithmetic and copies ran while one was open for 0% -> 1% of each run, Pallas kernels for 0% -> 0%
where the time goes in v1:
time: 774 us; the launch traced here: 769 us
  waiting for transfers between devices  357 us (46%)
  blocking collectives  346 us (45%)
  matrix products  23.7 us (3%)
  between operations  17.1 us (2%)
  local copies, waits for them, and re-layouts  13.7 us (2%)
  other arithmetic  11.1 us (1%)
    unnamed x3, blocking collectives  306 us
    all_gather x1, waiting for transfers between devices, on_device(): lax.all_gather(grad_share.astype(jnp.bfloat16), ('batch', 'hidden'), axis...  167 us
    psum x1, waiting for transfers between devices, on_device(): audio_part = lax.psum(partial_audio, 'hidden')  127 us
    all_gather x1, waiting for transfers between devices, on_device(): all_normed = lax.all_gather(normed, 'batch', axis=0, tiled=True)  48.7 us
    all_gather x1, blocking collectives, on_device(): all_stacked = lax.all_gather(masked, 'batch', axis=0, tiled=True)  21.6 us
  transfers between devices with their start and end apart: 4, of which 4 were waited for; matrix products, arithmetic and copies ran while one was open for 1% of the time, Pallas kernels for 0%

profile of v1, /device:TPU:1, one launch (start us, length us, event | category | flops | bytes accessed | tf_op | source)
XLA Modules:
  0.0 769.1 jit_solution(12971479772562971977)
XLA Ops:
  7.2 0.9 slice.43
  8.9 1.7 fusion.9
  12.0 2.8 convert_select_fusion
  14.8 126.9 %all-reduce.6.cloned.1.call-done = f32[64,4096]{1,0:T(8,128)} async-done(((f32[64,4096]{1,0:T(8,128)}), f32[64,4096]{1,0:T(8,128)}) %all-reduce.6.cloned.1.call-update) | async-done | bytes 1048592 | tf_op jit(solution)/shard_map/psum | solution.py:20
  141.7 2.1 slice_select_fusion
  143.8 1.0 copy-done.1
  145.3 8.9 %psum.15 = f32[128]{0:T(128)S(1)} all-reduce(f32[128]{0:T(128)S(1)} %multiply_reduce_fusion), channel_id=1, replica_groups=mesh['batch'=4,'hidden'=16,'width'=4] {'width'}, use_global_device_ids=true, to_apply=%region_2.3 | all-reduce | flops 128 | bytes 1024 | tf_op jit(solution)/shard_map/psum | solution.py:29
  154.2 2.8 multiply_convert_fusion
  157.1 48.7 %all-gather.4.cloned.1.call-done = bf16[512,4096]{1,0:T(8,128)(2,1)} async-done(((bf16[128,4096]{1,0:T(8,128)(2,1)}), bf16[512,4096]{1,0:T(8,128)(2,1)}) %all-gather.4.cloned.1.call-update) | async-done | bytes 4194320 | tf_op jit(solution)/shard_map/all_gather | solution.py:35
  205.8 9.1 %fusion.10 = f32[512,832]{0,1:T(8,128)} fusion(bf16[512,4096]{1,0:T(8,128)(2,1)} %all-gather.4.cloned.1.call-done, bf16[4096,832]{0,1:T(8,128)(2,1)} %bitcast.32), kind=kOutput, calls=%fused_computation.30 | convolution fusion | flops 3489660928 | bytes 12713984 | tf_op jit(solution)/shard_map/dot_general | solution.py:38
  218.9 6.7 all-reduce.1
  225.6 3.2 slice.63
  228.8 14.3 %reduce-scatter.2.cloned.1.call-done = f32[128,832]{0,1:T(8,128)} async-done(((f32[512,832]{0,1:T(8,128)}), f32[128,832]{0,1:T(8,128)}) %reduce-scatter.2.cloned.1.call-update) | async-done | bytes 426000 | tf_op jit(solution)/shard_map/reduce_scatter | solution.py:39
  243.1 1.7 add_divide_fusion
  244.9 1.2 add_reduce_fusion
  246.2 9.8 %all_gather.20 = bf16[256,832]{1,0:T(8,128)(2,1)S(1)} all-gather(bf16[64,832]{1,0:T(8,128)(2,1)S(1)} %copy.12), channel_id=1, replica_groups=mesh['batch'=4,'hidden'=16,'width'=4] {'width'}, dimensions={0}, use_global_device_ids=true | all-gather | bytes 532480 | tf_op jit(solution)/shard_map/all_gather | solution.py:51
  256.1 7.6 all-reduce
  263.7 8.1 %fusion.1 = f32[256,4096]{1,0:T(8,128)} fusion(bf16[256,832]{1,0:T(8,128)(2,1)S(1)} %all_gather.20, bf16[4096,832]{0,1:T(8,128)(2,1)} %bitcast.33, bf16[256,4096]{1,0:T(8,128)(2,1)} %bitcast.28, f32[256]{0:T(256)S(1)} %all-reduce.1, f32[256]{0:T(256)S(1)} %all-reduce, f32[4096]{0:T(1024)S(1)} %convert_element_type.26), kind=kOutput, calls=%fused_computation.2 | convolution fusion | flops 1751121920 | bytes 13551616 | tf_op jit(solution)/shard_map/dot_general | solution.py:53
  271.8 291.5 %all-reduce.7 = bf16[256,4096]{1,0:T(8,128)(2,1)} all-reduce(f32[256,4096]{1,0:T(8,128)} %fusion.1), channel_id=3, replica_groups=mesh['batch'=4,'hidden'=16,'width'=4] {'batch','hidden'}, use_global_device_ids=true, to_apply=%region_5.6.clone | all-reduce | flops 1048576 | bytes 6291456
  563.3 1.5 fusion.7
  564.8 21.6 %all_gather.19 = bf16[256,320]{1,0:T(8,128)(2,1)S(1)} all-gather(bf16[64,320]{1,0:T(8,128)(2,1)S(1)} %broadcast_select_fusion), channel_id=1, replica_groups=mesh['batch'=4,'hidden'=16,'width'=4] {'batch'}, dimensions={0}, use_global_device_ids=true | all-gather | bytes 204800 | tf_op jit(solution)/shard_map/all_gather | solution.py:33
  586.4 167.3 %all-gather.6.cloned.1.call-done = bf16[64,4,4096]{2,1,0:T(4,128)(2,1)} async-done(((bf16[1,4,4096]{2,1,0:T(4,128)(2,1)}), bf16[64,4,4096]{2,1,0:T(4,128)(2,1)}) %all-gather.6.cloned.1.call-update) | async-done | bytes 2097168 | tf_op jit(solution)/shard_map/all_gather | solution.py:60
  753.8 4.0 reshape.44
  757.7 4.8 fusion.11
  (40 shorter events, 3.9 us)
Async XLA Ops:
  7.2 1.8 copy-start
  7.2 4.8 copy-start.4
  7.2 134.5 %all-reduce.6.cloned.1.call-start = ((), (), s32[]{:S(2)}) async-start(), calls=%async_computation.1 | async-start | bytes 2097152 | tf_op jit(solution)/shard_map/psum | solution.py:20
  10.6 195.1 %all-gather.4.cloned.1.call-start = ((), (), s32[]{:S(2)}) async-start(), calls=%async_computation.2 | async-start | bytes 5242880 | tf_op jit(solution)/shard_map/all_gather | solution.py:35
  143.8 1.0 copy-start.1
  143.8 1.3 copy-start.2
  157.0 86.1 %reduce-scatter.2.cloned.1.call-start = ((), (), s32[]{:S(2)}) async-start(), calls=%async_computation.3 | async-start | bytes 2129920 | tf_op jit(solution)/shard_map/reduce_scatter | solution.py:39
  205.8 9.2 %copy-start.7 = (u32[256]{0:T(256)S(1)}, u32[256]{0:T(256)}, u32[]{:S(2)}) copy-start(u32[256]{0:T(256)} %constant.21) | copy-start | bytes 3076
  205.8 9.9 %copy-start.6 = (u32[256]{0:T(256)S(1)}, u32[256]{0:T(256)}, u32[]{:S(2)}) copy-start(u32[256]{0:T(256)} %constant.26) | copy-start | bytes 3076
  205.8 11.8 %copy-start.5 = (u32[256]{0:T(256)S(1)}, u32[256]{0:T(256)}, u32[]{:S(2)}) copy-start(u32[256]{0:T(256)} %constant.33) | copy-start | bytes 3076
  214.9 29.9 %copy-start.3 = (bf16[128,416]{0,1:T(8,128)(2,1)S(1)}, bf16[128,416]{0,1:T(8,128)(2,1)}, u32[]{:S(2)}) copy-start(bf16[128,416]{0,1:T(8,128)(2,1)} %param.15) | copy-start | bytes 319492
  214.9 538.8 %all-gather.6.cloned.1.call-start = ((), (), s32[]{:S(2)}) async-start(), calls=%async_computation.4 | async-start | bytes 2129920 | tf_op jit(solution)/shard_map/all_gather | solution.py:60
Sparse Core Ops, SparseCore 0:
  10.7 130.9 all-reduce.5
  157.1 48.5 all-gather.3
  215.0 28.0 reduce-scatter.1
  564.9 188.8 all-gather.5

commit v2 on v1

v2 whole, which is shorter than its diff:
```python
import jax
import jax.numpy as jnp
from jax import lax
from jax.experimental import pallas as pl
from jax.experimental.pallas import tpu as pltpu
from jax.sharding import PartitionSpec as P

D = 16384
HEAD = 64
PADDED = 896
CHUNKS = 2
norm_eps = 1e-05
MESH = pl.DeviceIdType.MESH
BF = jnp.bfloat16
F32 = jnp.float32


def fused_kernel(
    alen, tlen, stacked, kernel, text, gains, cot, w_hbm,
    hidden_out, grad_out, frames_out,
    w, xh, xt, pa, sta, rxa, stz, rza, gst, gown, grx, gall, bst, brx, xst, xown, xrx, zst, zrx,
    send_sems, recv_sems, local_sem,
):
    batch, hid, y = (lax.axis_index(a) for a in ("batch", "hidden", "width"))
    xhi, c = batch // 2, batch % 2
    xlo, z = hid // 8, hid % 8
    x = xhi * 2 + xlo
    width = text.shape[1]
    units = w_hbm.shape[0]
    half = units // 2
    span = width // CHUNKS
    part = span // 8

    def device(x_=x, c_=c, z_=z, y_=y):
        return {"batch": (x_ // 2) * 2 + c_, "hidden": (x_ % 2) * 8 + z_, "width": y_}

    def zmod(k):
        return lax.rem(z + k, 8)

    def xmod(k):
        return lax.rem(x + k, 4)

    def ymod(k):
        return lax.rem(y + k, 4)

    def slot(seq):
        return (seq % 2) * 2 + seq // 2

    sibling = device(c_=1 - c)
    pair = device(x_=xhi * 2 + 1 - xlo)
    cross = device(x_=(1 - xhi) * 2 + 1 - xlo)
    z_peers = [device(z_=zmod(k)) for k in range(1, 8)]
    x_peers = [device(x_=xmod(k)) for k in range(1, 4)]
    y_peers = [device(y_=ymod(k)) for k in range(1, 4)]

    barrier = pltpu.get_barrier_semaphore()
    peers = [sibling] + z_peers + x_peers + y_peers
    for p in peers:
        pl.semaphore_signal(barrier, inc=1, device_id=p, device_id_type=MESH)

    started = []

    def send(src, dst, peer):
        i = len(started)
        copy = pltpu.make_async_remote_copy(
            src_ref=src, dst_ref=dst, send_sem=send_sems.at[i], recv_sem=recv_sems.at[i],
            device_id=peer, device_id_type=MESH,
        )
        copy.start()
        started.append(copy)
        return copy

    w_copy = pltpu.make_async_copy(w_hbm, w.at[pl.ds(0, units)], local_sem)
    w_copy.start()

    def rows(start, size):
        return pl.ds(pl.multiple_of(start, size), size)

    def tiles(count, body):
        def step(i, carry):
            body(i)
            return carry

        lax.fori_loop(0, count, step, 0)

    def audio_tile(i):
        lanes = pl.ds(pl.multiple_of(i * 512, 512), 512)
        pa[:, lanes] = jnp.dot(stacked[...], kernel[:, lanes], preferred_element_type=F32)

    tiles(width // 512, audio_tile)
    sta[...] = pa[rows(32 * (1 - xlo), 32), :].astype(BF)

    pl.semaphore_wait(barrier, len(peers))
    pair_copies = []
    for j in range(CHUNKS):
        lanes = pl.ds(j * span, span)
        pair_copies.append(send(sta.at[:, lanes], rxa.at[:, lanes], pair))

    audio_count = alen[0]
    filled = alen[0] + tlen[0]
    head_pos = lax.broadcasted_iota(jnp.int32, (HEAD, 1), 0)
    me = slot(batch)
    frames_out[rows(me * HEAD, HEAD), :] = jnp.where(
        head_pos < audio_count, stacked[...], jnp.zeros_like(stacked[...])
    )

    def tail_tile(i):
        lanes = pl.ds(pl.multiple_of(i * 512, 512), 512)
        vals = text[HEAD:, lanes].astype(F32)
        keep = jnp.where((head_pos + HEAD) < filled, vals, 0.0)
        xt[rows(me * HEAD, HEAD), lanes] = (keep * gains[0:1, lanes]).astype(BF)

    tiles(width // 512, tail_tile)
    mine = rows(me * HEAD, HEAD)
    theirs = rows(slot((1 - xhi) * 2 + c) * HEAD, HEAD)
    cross_copy = send(xt.at[mine], xt.at[mine], cross)
    tail_sib = send(xt.at[mine], xt.at[mine], sibling)
    f_far = send(frames_out.at[mine], frames_out.at[mine], device(x_=(1 - xhi) * 2 + xlo))
    f_sib = send(frames_out.at[mine], frames_out.at[mine], sibling)

    own_rows = rows(32 * xlo, 32)

    def piece(j, who):
        return pl.ds(pl.multiple_of(j * span + who * part, part), part)

    z_copies = []
    for j in range(CHUNKS):
        pair_copies[j].wait_recv()
        lanes = pl.ds(j * span, span)
        pa[own_rows, lanes] = pa[own_rows, lanes] + rxa[:, lanes].astype(F32)
        stz[:, lanes] = pa[own_rows, lanes].astype(BF)
        z_copies.append([
            send(stz.at[:, piece(j, zmod(k))], rza.at[k - 1, :, pl.ds(j * part, part)], z_peers[k - 1])
            for k in range(1, 8)
        ])

    place = rows(c * 128 + x * 32, 32)
    pos = lax.broadcasted_iota(jnp.int32, (32, 1), 0) + 32 * xlo

    def gather_z(buf, j):
        lanes = piece(j, z)
        return [send(buf.at[place, lanes], buf.at[place, lanes], p) for p in z_peers]

    def gather_x(buf, j):
        lanes = pl.ds(j * span, span)
        xs = [send(buf.at[place, lanes], buf.at[place, lanes], p) for p in x_peers]
        return xs, [send(buf.at[place, lanes], buf.at[place, lanes], sibling)]

    def forward(buf, j, xs, sibs):
        lanes = pl.ds(j * span, span)
        for k in range(1, 4):
            xs[k - 1].wait_recv()
            there = rows(c * 128 + xmod(4 - k) * 32, 32)
            sibs.append(send(buf.at[there, lanes], buf.at[there, lanes], sibling))

    ag = []
    for j in range(CHUNKS):
        lanes = piece(j, z)
        total = pa[own_rows, lanes]
        for k in range(7):
            z_copies[j][k].wait_recv()
            total = total + rza[k, :, pl.ds(j * part, part)].astype(F32)
        words = text[own_rows, lanes].astype(F32)
        stream = jnp.where(pos < audio_count, total, jnp.where(pos < filled, words, 0.0))
        xh[place, lanes] = (stream * gains[0:1, lanes]).astype(BF)
        ag.append(gather_z(xh, j))
    xcop = []
    for j in range(CHUNKS):
        for cp in ag[j]:
            cp.wait_recv()
        xcop.append(gather_x(xh, j))

    cross_copy.wait_recv()
    tail_fwd = send(xt.at[theirs], xt.at[theirs], sibling)
    f_far.wait_recv()
    f_fwd = send(frames_out.at[theirs], frames_out.at[theirs], sibling)
    w_copy.wait()
    w[pl.ds(units, PADDED - units), :] = jnp.zeros((PADDED - units, width), BF)
    tail_sib.wait_recv()
    tail_fwd.wait_recv()

    lane = lax.broadcasted_iota(jnp.int32, (256, 128), 1)
    mark = units - (PADDED - 128)

    def project(buf, dst):
        def square(i, acc):
            lanes = pl.ds(pl.multiple_of(i * 128, 128), 128)
            v = buf[:, lanes].astype(F32) * gains[1:2, lanes]
            return acc + v * v

        sq = lax.fori_loop(0, width // 128, square, jnp.zeros((256, 128), F32))
        sq = jnp.sum(sq, axis=1, keepdims=True)
        high = sq.astype(BF).astype(F32)
        low = sq - high
        for start in range(0, PADDED, 256):
            size = min(256, PADDED - start)
            out = lax.dot_general(
                buf[...], w[pl.ds(start, size), :], (((1,), (1,)), ((), ())),
                preferred_element_type=F32,
            )
            if start + size == PADDED:
                out = jnp.where(lane == mark, high, jnp.where(lane == mark + 1, low, out))
            dst[:, pl.ds(start, size)] = out.astype(BF)
        return [
            send(dst.at[rows(slot(ymod(k)) * HEAD, HEAD)], grx.at[yslot(dst, k)], y_peers[k - 1])
            for k in range(1, 4)
        ]

    def yslot(dst, k):
        return (0 if dst is gst else 3) + k - 1

    tail_y = project(xt, gst)

    for j in range(CHUNKS):
        forward(xh, j, *xcop[j])
    for j in range(CHUNKS):
        for cp in xcop[j][1]:
            cp.wait_recv()
    head_y = project(xh, gown)

    for cp in tail_y + head_y:
        cp.wait_recv()
    keep = rows(slot(y) * HEAD, HEAD)

    def total_of(own, base):
        t = own[keep, :].astype(F32)
        for k in range(3):
            t = t + grx[base + k].astype(F32)
        return t

    both = jnp.concatenate([total_of(gown, 3), total_of(gst, 0)], axis=0).T
    stat = both[units : units + 8]
    inv = lax.rsqrt((stat[0:1] + stat[1:2]) / D + norm_eps)
    gate = both[:half] * inv
    up = both[half:units] * inv
    sig = jax.nn.sigmoid(gate)
    silu = gate * sig
    hidden_out[...] = (silu * up).astype(BF)
    cotv = cot[...].astype(F32)
    g_gate = cotv * up * sig * (1.0 + gate * (1.0 - sig))
    g_up = cotv * silu
    inner = jnp.sum(g_gate * gate + g_up * up, axis=0, keepdims=True) * (inv * inv) / D
    high = inner.astype(BF).astype(F32)
    row = lax.broadcasted_iota(jnp.int32, (PADDED - units, 128), 0)
    extra = jnp.where(row == 0, high, jnp.where(row == 1, inner - high, 0.0))
    grads = jnp.concatenate([g_gate * inv, g_up * inv, extra], axis=0).T
    gall[keep, :] = grads[:HEAD].astype(BF)
    for cp in [send(gall.at[keep], gall.at[keep], p) for p in y_peers]:
        cp.wait_recv()

    lane128 = lax.broadcasted_iota(jnp.int32, (128, 128), 1)

    def share(base, i):
        block = rows(base, 128)
        lanes = pl.ds(pl.multiple_of(i * 512, 512), 512)
        last = gall[block, pl.ds(PADDED - 128, 128)].astype(F32)
        marked = jnp.logical_or(lane128 == mark, lane128 == mark + 1)
        coef = jnp.sum(jnp.where(marked, last, 0.0), axis=1, keepdims=True)
        out = jnp.dot(gall[block, :], w[:, lanes], preferred_element_type=F32)
        return out * gains[0:1, lanes] - xh[block, lanes].astype(F32) * gains[1:2, lanes] * coef

    sib_copies = []
    for j in range(CHUNKS):
        def to_sibling(i, j=j):
            i = i + j * (span // 512)
            bst[:, pl.ds(pl.multiple_of(i * 512, 512), 512)] = share((1 - c) * 128, i).astype(BF)

        tiles(span // 512, to_sibling)
        lanes = pl.ds(j * span, span)
        sib_copies.append(send(bst.at[:, lanes], brx.at[:, lanes], sibling))
    x_copies = []
    for j in range(CHUNKS):
        sib_copies[j].wait_recv()

        def to_x(i, j=j):
            i = i + j * (span // 512)
            lanes = pl.ds(pl.multiple_of(i * 512, 512), 512)
            out = share(c * 128, i) + brx[:, lanes].astype(F32)
            xown[:, lanes] = out
            xst[:, lanes] = out.astype(BF)

        tiles(span // 512, to_x)
        lanes = pl.ds(j * span, span)
        x_copies.append([
            send(xst.at[rows(xmod(k) * 32, 32), lanes], xrx.at[k - 1, :, lanes], x_peers[k - 1])
            for k in range(1, 4)
        ])
    mine32 = rows(x * 32, 32)
    z_copies = []
    for j in range(CHUNKS):
        lanes = pl.ds(j * span, span)
        for cp in x_copies[j]:
            cp.wait_recv()
        out = xown[mine32, lanes]
        for k in range(3):
            out = out + xrx[k, :, lanes].astype(F32)
        xown[mine32, lanes] = out
        zst[:, lanes] = out.astype(BF)
        z_copies.append([
            send(zst.at[:, piece(j, zmod(k))], zrx.at[k - 1, :, pl.ds(j * part, part)], z_peers[k - 1])
            for k in range(1, 8)
        ])
    ag = []
    for j in range(CHUNKS):
        lanes = piece(j, z)
        total = xown[mine32, lanes]
        for k in range(7):
            z_copies[j][k].wait_recv()
            total = total + zrx[k, :, pl.ds(j * part, part)].astype(F32)
        grad_out[place, lanes] = total.astype(BF)
        ag.append(gather_z(grad_out, j))
    xcop = []
    for j in range(CHUNKS):
        for cp in ag[j]:
            cp.wait_recv()
        xcop.append(gather_x(grad_out, j))
    for j in range(CHUNKS):
        forward(grad_out, j, *xcop[j])
    for j in range(CHUNKS):
        for cp in xcop[j][1]:
            cp.wait_recv()
    f_sib.wait_recv()
    f_fwd.wait_recv()
    for cp in started:
        cp.wait_send()


COPIES = 140


def on_device(
    frames, adapter_weight, text_embed, audio_len, text_len, norm_gain, gate_up, cotangent
):
    feat_here = frames.shape[2]
    width_here = adapter_weight.shape[2]
    units = 2 * gate_up.shape[2]
    depth = 4 * feat_here
    stacked = frames[0, : 4 * HEAD].reshape(HEAD, depth)
    kernel = adapter_weight.reshape(depth, width_here)
    gain = norm_gain.astype(F32)
    gains = jnp.stack([gain, 1.0 / gain])
    weights = jnp.transpose(gate_up, (1, 2, 0)).reshape(units, width_here)
    cot = cotangent.T
    vmem = pl.BlockSpec(memory_space=pltpu.VMEM)
    smem = pl.BlockSpec(memory_space=pltpu.SMEM)
    scratch = [
        ((PADDED, width_here), BF),
        ((256, width_here), BF),
        ((256, width_here), BF),
        ((HEAD, width_here), F32),
        ((32, width_here), BF),
        ((32, width_here), BF),
        ((32, width_here), BF),
        ((7, 32, width_here // 8), BF),
        ((256, PADDED), BF),
        ((256, PADDED), BF),
        ((6, HEAD, PADDED), BF),
        ((256, PADDED), BF),
        ((128, width_here), BF),
        ((128, width_here), BF),
        ((128, width_here), BF),
        ((128, width_here), F32),
        ((3, 32, width_here), BF),
        ((32, width_here), BF),
        ((7, 32, width_here // 8), BF),
    ]
    hidden, grad, all_frames = pl.pallas_call(
        fused_kernel,
        out_shape=(
            jax.ShapeDtypeStruct((units // 2, 128), BF),
            jax.ShapeDtypeStruct((256, width_here), BF),
            jax.ShapeDtypeStruct((256, depth), BF),
        ),
        in_specs=[smem, smem] + [vmem] * 5 + [pl.BlockSpec(memory_space=pl.ANY)],
        out_specs=(vmem, vmem, vmem),
        scratch_shapes=[pltpu.VMEM(s, t) for s, t in scratch]
        + [
            pltpu.SemaphoreType.DMA((COPIES,)),
            pltpu.SemaphoreType.DMA((COPIES,)),
            pltpu.SemaphoreType.DMA,
        ],
        compiler_params=pltpu.CompilerParams(
            collective_id=0, has_side_effects=True, vmem_limit_bytes=56 << 20
        ),
    )(audio_len, text_len, stacked, kernel, text_embed, gains, cot, weights)
    weight_grad = lax.dot_general(
        all_frames, grad, (((0,), (0,)), ((), ())), preferred_element_type=F32
    )
    return (hidden.T, weight_grad.reshape(4, feat_here, width_here))


def solution(mesh):
    return jax.shard_map(
        on_device,
        mesh=mesh,
        in_specs=(
            P("batch", None, "hidden"),
            P(None, "hidden", "width"),
            P("batch", "width"),
            P("batch"),
            P("batch"),
            P("width"),
            P("width", None, ("batch", "hidden")),
            P("width", ("batch", "hidden")),
        ),
        out_specs=(P("width", ("batch", "hidden")), P(None, "hidden", "width")),
        check_vma=False,
    )
```

time: 774 us -> 120 us (0.16)
  waiting for transfers between devices: 357 us -> 0 us
  blocking collectives: 346 us -> 0 us
  Pallas kernels: 0 us -> 108 us
  matrix products: 23.7 us -> 4.97 us
  between operations: 17.1 us -> 1.95 us
  local copies, waits for them, and re-layouts: 13.7 us -> 2.28 us
  other arithmetic: 11.1 us -> 2.06 us
    unnamed x3 -> x0, blocking collectives: 306 us -> none
    all_gather x2 -> x0, waiting for transfers between devices: 216 us -> none  [the longest x1 167 us: on_device(): lax.all_gather(grad_share.astype(jnp.bfloat16), ('batch', 'hidden'), axis...]
    psum x1 -> x0, waiting for transfers between devices: 127 us -> none  [on_device(): audio_part = lax.psum(partial_audio, 'hidden')]
    pallas_call x0 -> x1, Pallas kernels: none -> 108 us  [on_device(): pl.pallas_call(fused_kernel, out_shape=(jax.ShapeDtypeStruct((units // 2,...]
    all_gather x2 -> x0, blocking collectives: 31.3 us -> none  [the longest x1 21.6 us: on_device(): all_stacked = lax.all_gather(masked, 'batch', axis=0, tiled=True)]
    dot_general x4 -> x1, matrix products: 23.7 us -> 4.97 us  [on_device(): lax.dot_general(all_frames, grad, (((0,), (0,)), ((), ())), preferred_ele...]
    reduce_scatter x1 -> x0, waiting for transfers between devices: 14.3 us -> none  [on_device(): lax.psum_scatter(partial_pair, 'width', scatter_dimension=0, tiled=True)]
    psum x1 -> x0, blocking collectives: 8.85 us -> none  [on_device(): sum_squares = lax.psum(jnp.sum(stream * stream, axis=1), 'width')]
  transfers between devices with their start and end apart: 4 -> 0, of which waited for: 4 -> 0; matrix products, arithmetic and copies ran while one was open for 1% -> 0% of each run, Pallas kernels for 0% -> 0%
where the time goes in v2:
time: 120 us
  Pallas kernels  108 us (90%)
  matrix products  4.97 us (4%)
  local copies, waits for them, and re-layouts  2.28 us (2%)
  other arithmetic  2.06 us (2%)
  between operations  1.95 us (2%)
    pallas_call x1, Pallas kernels, on_device(): pl.pallas_call(fused_kernel, out_shape=(jax.ShapeDtypeStruct((units // 2,...  108 us
    dot_general x1, matrix products, on_device(): lax.dot_general(all_frames, grad, (((0,), (0,)), ((), ())), preferred_ele...  4.97 us

profile of v2, /device:TPU:1, one launch (start us, length us, event | category | flops | bytes accessed | tf_op | source)
XLA Modules:
  0.0 119.6 jit_solution(920967314581573782)
XLA Ops:
  1.9 0.7 broadcast_divide_fusion
  2.6 0.7 convert_element_type.3
  3.3 0.6 pad_maximum_fusion.gains
  4.0 0.8 slice.3
  4.8 0.1 copy.11
  4.9 0.7 reshape_squeeze.3.stacked
  5.6 108.4 %shard_map.95 = (bf16[416,128]{1,0:T(8,128)(2,1)}, bf16[256,4096]{1,0:T(8,128)(2,1)}, bf16[256,320]{1,0:T(8,128)(2,1)}) custom-call(s32[1]{0:T(128)S(6)} %copy.13.alen, s32[1]{0:T(128)S(6)} %copy.14.tlen, bf16[64,320]{1,0:T(8,128)(2,1)} %reshape_squeeze.3.stacked, bf16[320,4096]{1,0:T(8,128)(2,1)} %bitcast.13, bf16[128,4096]{1,0:T(8,128)(2,1)} %text.1, ...), custom_call_target="tpu_custom_call" | custom-call | tf_op jit(solution)/shard_map/pallas_call | solution.py:367
  114.0 0.0 copy-start
  114.0 5.0 %fusion = f32[320,4096]{1,0:T(8,128)} fusion(bf16[256,320]{1,0:T(8,128)(2,1)} %get-tuple-element.6, bf16[256,4096]{1,0:T(8,128)(2,1)} %get-tuple-element.7), kind=kOutput, calls=%fused_computation.2 | convolution fusion | flops 671088640 | bytes 7503872 | tf_op jit(solution)/shard_map/dot_general | solution.py:386
  119.0 0.0 copy-done
  119.0 0.6 copy.15
Async XLA Ops:
  114.0 5.0 %copy-start = (bf16[416,128]{1,0:T(8,128)(2,1)S(1)}, bf16[416,128]{1,0:T(8,128)(2,1)}, u32[]{:S(2)}) copy-start(bf16[416,128]{1,0:T(8,128)(2,1)} %get-tuple-element.5) | copy-start | bytes 319492

commit v3 on v1

v3 whole, which is shorter than its diff:
```python
import jax
import jax.numpy as jnp
from jax import lax
from jax.experimental import pallas as pl
from jax.experimental.pallas import tpu as pltpu
from jax.sharding import PartitionSpec as P

D = 16384
HEAD = 64
PADDED = 896
CHUNKS = 4
COPIES = 96
norm_eps = 1e-05
MESH = pl.DeviceIdType.MESH
BF = jnp.bfloat16
F32 = jnp.float32
SUMS_A = BF
SUMS_B = F32


def fused_kernel(
    alen, tlen, frames, kernel, text, gain, cot, w_hbm,
    hidden_out, grad_out, frames_out,
    gains, w, xh, xt, taps, frm, pa, sta, rxa, stz, rza, stat_out, stat_in, gacc, tacc, sqs, gst, tst, grx,
    totals, gall, coefs, bst, brx, xst, xown, xrx, zst, zrx,
    send_sems, recv_sems, local_sem,
):
    batch, hid, y = (lax.axis_index(a) for a in ("batch", "hidden", "width"))
    xhi, c = batch // 2, batch % 2
    xlo, z = hid // 8, hid % 8
    x = xhi * 2 + xlo
    width = text.shape[1]
    feat = kernel.shape[1]
    units = w_hbm.shape[0]
    half = units // 2
    span = width // CHUNKS
    part = span // 8

    def device(x_=x, c_=c, z_=z, y_=y):
        return {"batch": (x_ // 2) * 2 + c_, "hidden": (x_ % 2) * 8 + z_, "width": y_}

    def zmod(k):
        return lax.rem(z + k, 8)

    def xmod(k):
        return lax.rem(x + k, 4)

    def ymod(k):
        return lax.rem(y + k, 4)

    def slot(seq):
        return (seq % 2) * 2 + seq // 2

    sibling = device(c_=1 - c)
    pair = device(x_=xhi * 2 + 1 - xlo)
    cross = device(x_=(1 - xhi) * 2 + 1 - xlo)
    far = device(x_=(1 - xhi) * 2 + xlo)
    z_peers = [device(z_=zmod(k)) for k in range(1, 8)]
    x_peers = [device(x_=xmod(k)) for k in range(1, 4)]
    y_peers = [device(y_=ymod(k)) for k in range(1, 4)]

    barrier = pltpu.get_barrier_semaphore()
    peers = [sibling] + z_peers + x_peers + y_peers
    for p in peers:
        pl.semaphore_signal(barrier, inc=1, device_id=p, device_id_type=MESH)

    groups = []
    landed = set()

    def group(ref, copies):
        i = len(groups)

        def describe(src, dst, peer):
            return pltpu.make_async_remote_copy(
                src_ref=src, dst_ref=dst, send_sem=send_sems.at[i], recv_sem=recv_sems.at[i],
                device_id=peer, device_id_type=MESH,
            )

        for src, dst, peer in copies:
            describe(src, dst, peer).start()
        groups.append(describe(ref, ref, copies[0][2]))
        return i

    def send(src, dst, peer):
        return group(dst, [(src, dst, peer)])

    def arrive(i):
        if i not in landed:
            landed.add(i)
            groups[i].wait_recv()

    def arrive_local():
        if "w" not in landed:
            landed.add("w")
            w_copy.wait()

    def finish():
        arrive_local()
        for i in range(len(groups)):
            arrive(i)
        for copy in groups:
            copy.wait_send()

    w_copy = pltpu.make_async_copy(w_hbm, w.at[pl.ds(0, units)], local_sem)
    w_copy.start()

    def rows(start, size):
        return pl.ds(pl.multiple_of(start, size), size)

    def columns(j):
        return pl.ds(j * span, span)

    def piece(j, who):
        return pl.ds(pl.multiple_of(j * span + who * part, part), part)

    def tiles(count, body):
        def step(i, carry):
            body(i)
            return carry

        lax.fori_loop(0, count, step, 0)

    def lanes_of(i, size):
        return pl.ds(pl.multiple_of(i * size, size), size)

    want = lax.broadcasted_iota(jnp.int32, (4 * HEAD, 4 * HEAD), 0)
    have = lax.broadcasted_iota(jnp.int32, (4 * HEAD, 4 * HEAD), 1)
    pick = jnp.where(have == 4 * (want % HEAD) + want // HEAD, 1.0, 0.0).astype(BF)
    taps[...] = lax.dot_general(
        pick, frames[:, 0 : 4 * HEAD], (((1,), (1,)), ((), ())), preferred_element_type=F32
    ).astype(BF)

    def audio_tile(i):
        lanes = lanes_of(i, 512)
        out = jnp.dot(taps[0:HEAD], kernel[0, :, lanes], preferred_element_type=F32)
        for tap in range(1, 4):
            out += jnp.dot(
                taps[tap * HEAD : (tap + 1) * HEAD], kernel[tap, :, lanes], preferred_element_type=F32
            )
        pa[:, lanes] = out

    own_rows = rows(32 * xlo, 32)
    other_rows = rows(32 * (1 - xlo), 32)
    pair_copies = []
    for j in range(CHUNKS):
        for i in range(span // 512):
            audio_tile(j * (span // 512) + i)
        sta[:, columns(j)] = pa[other_rows, columns(j)].astype(BF)
        if j == 0:
            pl.semaphore_wait(barrier, len(peers))
        pair_copies.append(send(sta.at[:, columns(j)], rxa.at[:, columns(j)], pair))

    audio_count = alen[0]
    filled = alen[0] + tlen[0]
    me = slot(batch)
    mine = rows(me * HEAD, HEAD)
    theirs = rows(slot((1 - xhi) * 2 + c) * HEAD, HEAD)

    def square(i, acc):
        v = text[:, lanes_of(i, 128)].astype(F32)
        return acc + v * v

    squares = lax.fori_loop(0, width // 128, square, jnp.zeros((128, 128), F32))
    squares = jnp.broadcast_to(jnp.sum(squares, axis=1, keepdims=True), (128, 128))
    stat_out[...] = squares.T[:8]
    stat_copies = group(stat_in, [(stat_out, stat_in.at[k - 1], y_peers[k - 1]) for k in range(1, 4)])
    head_pos = lax.broadcasted_iota(jnp.int32, (HEAD, 1), 0)
    lane64 = lax.broadcasted_iota(jnp.int32, (HEAD, 128), 1)
    is_audio = head_pos < audio_count
    frm[mine, :] = jnp.where(
        jnp.logical_and(is_audio, lax.broadcasted_iota(jnp.int32, (HEAD, 512), 1) == 127), 1.0, 0.0
    ).astype(BF)
    for tap in range(4):
        block = taps[tap * HEAD : (tap + 1) * HEAD]
        frm[mine, tap * 128 : tap * 128 + feat] = jnp.where(is_audio, block, jnp.zeros_like(block))
    f_far = send(frm.at[mine], frm.at[mine], far)
    f_sib = send(frm.at[mine], frm.at[mine], sibling)
    gain_vals = gain[...].astype(F32)
    for i in range(width // 128):
        gains[0:1, i * 128 : (i + 1) * 128] = gain_vals[i : i + 1]
    gains[1:2, :] = 1.0 / gains[0:1, :]
    arrive(stat_copies)
    stat = stat_out[...] + stat_in[0] + stat_in[1] + stat_in[2]
    inv_text = lax.rsqrt(stat[0:1] / D + norm_eps)
    inv_text = jnp.broadcast_to(inv_text, (128, 128)).T
    totals[:, 0:128] = inv_text

    place = rows(c * 128 + x * 32, 32)
    pos = lax.broadcasted_iota(jnp.int32, (32, 1), 0) + 32 * xlo

    def gather_z(buf, j):
        own = buf.at[place, piece(j, z)]
        return group(buf.at[place, pl.ds(j * span, 7 * part)], [(own, own, p) for p in z_peers])

    def gather_x(buf, j):
        own = buf.at[place, columns(j)]
        right = send(own, own, x_peers[0])
        left = send(own, own, x_peers[2])
        direct = send(own, own, x_peers[1]) if j == CHUNKS - 1 else None
        return right, left, direct

    def hand_on(buf, j, right, left, direct):
        before = c * 128 + xmod(3) * 32
        after = c * 128 + xmod(1) * 32
        arrive(right)
        arrive(left)
        if direct is None:
            low = buf.at[rows(before, 16), columns(j)]
            high = buf.at[rows(after + 16, 16), columns(j)]
            both = buf.at[rows(c * 128 + xmod(2) * 32, 32), columns(j)]
            direct = group(both, [(low, low, x_peers[0]), (high, high, x_peers[2])])
        return direct

    def to_core(buf, j, direct):
        arrive(direct)
        half_rows = buf.at[rows(c * 128, 128), columns(j)]
        return send(half_rows, half_rows, sibling)

    def scatter_z(stage, landing, j):
        lanes = pl.ds(j * part, part)
        return group(
            landing.at[:, :, lanes],
            [(stage.at[:, piece(j, zmod(k))], landing.at[k - 1, :, lanes], z_peers[k - 1]) for k in range(1, 8)],
        )

    def pipeline(buf, order, first, second, last, extra):
        live = {}
        for t in range(CHUNKS + max(lag for _, lag in order)):
            for stage, lag in order:
                j = t - lag
                if j < 0 or j >= CHUNKS:
                    continue
                if stage == 0:
                    live[j] = first(j)
                elif stage == 1:
                    second(j, live[j])
                    live[j] = gather_z(buf, j)
                elif stage == 2:
                    arrive(live[j])
                    live[j] = gather_x(buf, j)
                elif stage == 3:
                    live[j] = hand_on(buf, j, *live[j])
                elif stage == 4:
                    live[j] = to_core(buf, j, live[j])
                else:
                    arrive(live[j])
                    last(j)
            extra(t)

    def pair_sum(j):
        arrive(pair_copies[j])
        out = pa[own_rows, columns(j)] + rxa[:, columns(j)].astype(F32)
        pa[own_rows, columns(j)] = out
        stz[:, columns(j)] = out.astype(stz.dtype)
        return scatter_z(stz, rza, j)

    def head_stream(j, copies):
        arrive(copies)
        lanes = piece(j, z)
        total = pa[own_rows, lanes]
        for k in range(7):
            total = total + rza[k, :, pl.ds(j * part, part)].astype(F32)
        words = text[own_rows, lanes].astype(F32) * totals[own_rows, 0:1]
        stream = jnp.where(pos < audio_count, total, jnp.where(pos < filled, words, 0.0))
        xh[place, lanes] = (stream * gains[0:1, lanes]).astype(BF)

    def project(buf, acc, j):
        lanes = columns(j)
        for start in range(0, PADDED, 256):
            size = min(256, PADDED - start)
            out = lax.dot_general(
                buf[:, lanes], w[pl.ds(start, size), lanes], (((1,), (1,)), ((), ())),
                preferred_element_type=F32,
            )
            if j == 0:
                acc[:, pl.ds(start, size)] = out
            else:
                acc[:, pl.ds(start, size)] += out

    def head_project(j):
        if j == 0:
            arrive_local()
            w[pl.ds(units, PADDED - units), :] = jnp.zeros((PADDED - units, width), BF)
            sqs[...] = jnp.zeros_like(sqs)

        def head_square(i, carry):
            lanes = lanes_of(j * (span // 128) + i, 128)
            v = xh[:, lanes].astype(F32) * gains[1:2, lanes]
            sqs[...] += v * v
            return carry

        lax.fori_loop(0, span // 128, head_square, 0)
        project(xh, gacc, j)

    def tail_tile(i):
        lanes = lanes_of(i, 512)
        vals = text[HEAD:, lanes].astype(F32) * totals[HEAD:, 0:1]
        xt[mine, lanes] = (jnp.where((head_pos + HEAD) < filled, vals, 0.0) * gains[0:1, lanes]).astype(BF)

    def during_head(t):
        if t == CHUNKS:
            tiles(width // 512, tail_tile)

    pipeline(xh, ((1, 2), (0, 0), (2, 3), (3, 4), (4, 5), (5, 6)), pair_sum, head_stream, head_project, during_head)
    lane256 = lax.broadcasted_iota(jnp.int32, (256, 128), 1)
    mark = units - (PADDED - 128)
    last_tile = pl.ds(PADDED - 128, 128)
    sq = jnp.sum(sqs[...], axis=1, keepdims=True)
    high = sq.astype(BF).astype(F32)
    gacc[:, last_tile] = jnp.where(
        lane256 == mark, high, jnp.where(lane256 == mark + 1, sq - high, gacc[:, last_tile])
    )

    def spread(acc, stage, base):
        stage[...] = acc[...].astype(BF)
        return group(
            grx.at[base : base + 3],
            [
                (stage.at[rows(slot(ymod(k)) * HEAD, HEAD)], grx.at[base + k - 1], y_peers[k - 1])
                for k in (2, 1, 3)
            ],
        )

    head_y = spread(gacc, gst, 0)
    cross_copy = send(xt.at[mine], xt.at[mine], cross)
    tail_sib = send(xt.at[mine], xt.at[mine], sibling)
    arrive(f_far)
    f_fwd = send(frm.at[theirs], frm.at[theirs], sibling)
    arrive(f_sib)
    arrive(f_fwd)
    arrive(head_y)

    keep = rows(slot(y) * HEAD, HEAD)

    def total_of(acc, base):
        t = acc[keep, :]
        for k in range(3):
            t = t + grx[base + k].astype(F32)
        return t

    totals[0:HEAD, :] = total_of(gacc, 0)
    totals[HEAD:, :] = jnp.zeros((128 - HEAD, PADDED), F32)
    flag = frm[keep, 0:128].astype(F32)[:, 127:128]
    totals[0:HEAD, last_tile] = jnp.where(lane64 == mark + 2, flag, totals[0:HEAD, last_tile])

    def activations():
        both = totals[...].T
        stat = both[units : units + 8]
        inv = jnp.where(stat[2:3] > 0.5, lax.rsqrt((stat[0:1] + stat[1:2]) / D + norm_eps), 1.0)
        gate = both[:half] * inv
        up = both[half:units] * inv
        sig = jax.nn.sigmoid(gate)
        return inv, gate, up, sig, gate * sig

    inv, gate, up, sig, silu = activations()
    cotv = cot[...].astype(F32)
    g_gate = cotv * up * sig * (1.0 + gate * (1.0 - sig))
    g_up = cotv * silu
    inner = jnp.sum(g_gate * gate + g_up * up, axis=0, keepdims=True) * (inv * inv) / D
    high = inner.astype(BF).astype(F32)
    row = lax.broadcasted_iota(jnp.int32, (PADDED - units, 128), 0)
    extra_rows = jnp.where(row == 0, high, jnp.where(row == 1, inner - high, 0.0))
    grads = jnp.concatenate([g_gate * inv, g_up * inv, extra_rows], axis=0).T
    gall[keep, :] = grads[:HEAD].astype(BF)
    g_copies = group(gall.at[0 : 3 * HEAD], [(gall.at[keep], gall.at[keep], p) for p in y_peers])
    frames_t = frm[...].T
    for tap in range(4):
        frames_out[tap * feat : (tap + 1) * feat] = frames_t[tap * 128 : tap * 128 + feat]
    arrive(g_copies)

    edge = gall[:, last_tile].astype(F32)
    marked = jnp.logical_or(lane256 == mark, lane256 == mark + 1)
    coefs[...] = jnp.broadcast_to(
        jnp.sum(jnp.where(marked, edge, 0.0), axis=1, keepdims=True), (256, 128)
    )

    def share(base, lanes):
        block = rows(base, 128)
        out = jnp.dot(gall[block, :], w[:, lanes], preferred_element_type=F32)
        unit = xh[block, lanes].astype(F32) * gains[1:2, lanes]
        return out * gains[0:1, lanes] - unit * coefs[block, 0:1]

    sib_copies, x_copies = {}, {}

    def to_sibling(j):
        def tile(i):
            lanes = lanes_of(j * (span // 512) + i, 512)
            bst[:, lanes] = share((1 - c) * 128, lanes).astype(BF)

        tiles(span // 512, tile)
        sib_copies[j] = send(bst.at[:, columns(j)], brx.at[:, columns(j)], sibling)

    def to_x(j):
        arrive(sib_copies[j])

        def tile(i):
            lanes = lanes_of(j * (span // 512) + i, 512)
            out = share(c * 128, lanes) + brx[:, lanes].astype(F32)
            xown[:, lanes] = out
            xst[:, lanes] = out.astype(BF)

        tiles(span // 512, tile)
        x_copies[j] = group(
            xrx.at[:, :, columns(j)],
            [
                (xst.at[rows(xmod(k) * 32, 32), columns(j)], xrx.at[k - 1, :, columns(j)], x_peers[k - 1])
                for k in (2, 1, 3)
            ],
        )

    to_sibling(0)
    for j in range(CHUNKS):
        if j + 1 < CHUNKS:
            to_sibling(j + 1)
        to_x(j)
    arrive(cross_copy)
    tail_fwd = send(xt.at[theirs], xt.at[theirs], sibling)
    mine32 = rows(x * 32, 32)

    def x_sum(j):
        arrive(x_copies[j])
        out = xown[mine32, columns(j)]
        for k in range(3):
            out = out + xrx[k, :, columns(j)].astype(F32)
        xown[mine32, columns(j)] = out
        zst[:, columns(j)] = out.astype(zst.dtype)
        return scatter_z(zst, zrx, j)

    def head_grad(j, copies):
        arrive(copies)
        lanes = piece(j, z)
        total = xown[mine32, lanes]
        for k in range(7):
            total = total + zrx[k, :, pl.ds(j * part, part)].astype(F32)
        grad_out[place, lanes] = total.astype(BF)

    tail_y = []

    def during_tail(t):
        if t < CHUNKS:
            if t == 0:
                arrive(tail_sib)
                arrive(tail_fwd)
            project(xt, tacc, t)
        if t == CHUNKS - 1:
            tail_y.append(spread(tacc, tst, 3))
        if t == CHUNKS + 2:
            arrive(tail_y[0])
            totals[HEAD:, :] = total_of(tacc, 3)
            _, _, up, _, silu = activations()
            hidden_out[...] = (silu * up).astype(BF)

    pipeline(grad_out, ((0, 0), (1, 1), (2, 2), (3, 3), (4, 4), (5, 5)), x_sum, head_grad, lambda j: None, during_tail)
    finish()


def weight_kernel(frames_t, grad, out):
    feat = out.shape[1]
    total = jnp.dot(frames_t[...], grad[...], preferred_element_type=F32)
    for tap in range(4):
        out[tap] = total[tap * feat : (tap + 1) * feat]


def on_device(
    frames, adapter_weight, text_embed, audio_len, text_len, norm_gain, gate_up, cotangent
):
    feat_here = frames.shape[2]
    width_here = adapter_weight.shape[2]
    units = 2 * gate_up.shape[2]
    depth = 4 * feat_here
    gain = norm_gain.reshape(width_here // 128, 128)
    weights = jnp.transpose(gate_up, (1, 2, 0)).reshape(units, width_here)
    cot = cotangent.T
    vmem = pl.BlockSpec(memory_space=pltpu.VMEM)
    smem = pl.BlockSpec(memory_space=pltpu.SMEM)
    scratch = [
        ((2, width_here), F32),
        ((PADDED, width_here), BF),
        ((256, width_here), BF),
        ((256, width_here), BF),
        ((4 * HEAD, feat_here), BF),
        ((256, 512), BF),
        ((HEAD, width_here), F32),
        ((32, width_here), BF),
        ((32, width_here), BF),
        ((32, width_here), SUMS_A),
        ((7, 32, width_here // 8), SUMS_A),
        ((8, 128), F32),
        ((3, 8, 128), F32),
        ((256, PADDED), F32),
        ((256, PADDED), F32),
        ((256, 128), F32),
        ((256, PADDED), BF),
        ((256, PADDED), BF),
        ((6, HEAD, PADDED), BF),
        ((128, PADDED), F32),
        ((256, PADDED), BF),
        ((256, 128), F32),
        ((128, width_here), BF),
        ((128, width_here), BF),
        ((128, width_here), BF),
        ((128, width_here), F32),
        ((3, 32, width_here), BF),
        ((32, width_here), SUMS_B),
        ((7, 32, width_here // 8), SUMS_B),
    ]
    hidden, grad, frames_t = pl.pallas_call(
        fused_kernel,
        out_shape=(
            jax.ShapeDtypeStruct((units // 2, 128), BF),
            jax.ShapeDtypeStruct((256, width_here), BF),
            jax.ShapeDtypeStruct((depth, 256), BF),
        ),
        in_specs=[smem, smem] + [vmem] * 5 + [pl.BlockSpec(memory_space=pl.ANY)],
        out_specs=(vmem, vmem, vmem),
        scratch_shapes=[pltpu.VMEM(s, t) for s, t in scratch]
        + [
            pltpu.SemaphoreType.DMA((COPIES,)),
            pltpu.SemaphoreType.DMA((COPIES,)),
            pltpu.SemaphoreType.DMA,
        ],
        compiler_params=pltpu.CompilerParams(
            collective_id=0, has_side_effects=True, vmem_limit_bytes=56 << 20
        ),
    )(audio_len, text_len, frames[0].T, adapter_weight, text_embed, gain, cot, weights)
    tile = width_here // 4
    weight_grad = pl.pallas_call(
        weight_kernel,
        grid=(width_here // tile,),
        out_shape=jax.ShapeDtypeStruct((4, feat_here, width_here), F32),
        in_specs=[
            pl.BlockSpec((depth, 256), lambda i: (0, 0)),
            pl.BlockSpec((256, tile), lambda i: (0, i)),
        ],
        out_specs=pl.BlockSpec((4, feat_here, tile), lambda i: (0, 0, i)),
    )(frames_t, grad)
    return (hidden.T, weight_grad)


def solution(mesh):
    return jax.shard_map(
        on_device,
        mesh=mesh,
        in_specs=(
            P("batch", None, "hidden"),
            P(None, "hidden", "width"),
            P("batch", "width"),
            P("batch"),
            P("batch"),
            P("width"),
            P("width", None, ("batch", "hidden")),
            P("width", ("batch", "hidden")),
        ),
        out_specs=(P("width", ("batch", "hidden")), P(None, "hidden", "width")),
        check_vma=False,
    )
```

time: 774 us -> 111 us (0.14)
  waiting for transfers between devices: 357 us -> 0 us
  blocking collectives: 346 us -> 0 us
  Pallas kernels: 0 us -> 108 us
  matrix products: 23.7 us -> 0 us
  between operations: 17.1 us -> 1.94 us
  local copies, waits for them, and re-layouts: 13.7 us -> 0.65 us
  other arithmetic: 11.1 us -> 0 us
    unnamed x3 -> x0, blocking collectives: 306 us -> none
    all_gather x2 -> x0, waiting for transfers between devices: 216 us -> none  [the longest x1 167 us: on_device(): lax.all_gather(grad_share.astype(jnp.bfloat16), ('batch', 'hidden'), axis...]
    psum x1 -> x0, waiting for transfers between devices: 127 us -> none  [on_device(): audio_part = lax.psum(partial_audio, 'hidden')]
    pallas_call x0 -> x2, Pallas kernels: none -> 108 us  [the longest x1 103 us: on_device(): pl.pallas_call(fused_kernel, out_shape=(jax.ShapeDtypeStruct((units // 2,...]
    all_gather x2 -> x0, blocking collectives: 31.3 us -> none  [the longest x1 21.6 us: on_device(): all_stacked = lax.all_gather(masked, 'batch', axis=0, tiled=True)]
    dot_general x4 -> x0, matrix products: 23.7 us -> none  [the longest x1 9.14 us: on_device(): jnp.dot(all_normed, weights, preferred_element_type=jnp.float32)]
    reduce_scatter x1 -> x0, waiting for transfers between devices: 14.3 us -> none  [on_device(): lax.psum_scatter(partial_pair, 'width', scatter_dimension=0, tiled=True)]
    psum x1 -> x0, blocking collectives: 8.85 us -> none  [on_device(): sum_squares = lax.psum(jnp.sum(stream * stream, axis=1), 'width')]
  transfers between devices with their start and end apart: 4 -> 0, of which waited for: 4 -> 0; matrix products, arithmetic and copies ran while one was open for 1% -> 0% of each run, Pallas kernels for 0% -> 0%
where the time goes in v3:
time: 111 us
  Pallas kernels  108 us (97%)
  between operations  1.94 us (2%)
    pallas_call x1, Pallas kernels, on_device(): pl.pallas_call(fused_kernel, out_shape=(jax.ShapeDtypeStruct((units // 2,...  103 us
    pallas_call x1, Pallas kernels, on_device(): pl.pallas_call(weight_kernel, grid=(width_here // tile,), out_shape=jax.S...  5 us

profile of v3, /device:TPU:1, one launch (start us, length us, event | category | flops | bytes accessed | tf_op | source)
XLA Modules:
  0.0 111.0 jit_solution(8368423383979668050)
XLA Ops:
  1.9 103.5 %shard_map.95 = (bf16[416,128]{1,0:T(8,128)(2,1)}, bf16[256,4096]{1,0:T(8,128)(2,1)}, bf16[320,256]{1,0:T(8,128)(2,1)}) custom-call(s32[1]{0:T(128)S(6)} %copy.11.alen, s32[1]{0:T(128)S(6)} %copy.12.tlen, bf16[80,512]{1,0:T(8,128)(2,1)} %bitcast.12, bf16[4,80,4096]{2,1,0:T(8,128)(2,1)} %kernel.1, bf16[128,4096]{1,0:T(8,128)(2,1)} %text.1, ...), custom_call_target="tpu_custom_call" | custom-call | tf_op jit(solution)/shard_map/pallas_call | solution.py:507
  105.4 0.0 copy-start
  105.4 5.0 %shard_map.96 = f32[4,80,4096]{2,1,0:T(8,128)} custom-call(bf16[320,256]{1,0:T(8,128)(2,1)} %get-tuple-element.6.frames_t, bf16[256,4096]{1,0:T(8,128)(2,1)} %get-tuple-element.7.grad), custom_call_target="tpu_custom_call" | custom-call | tf_op jit(solution)/shard_map/pallas_call | solution.py:527
  110.4 0.0 copy-done
  110.4 0.6 copy.13
Async XLA Ops:
  105.4 5.0 %copy-start = (bf16[416,128]{1,0:T(8,128)(2,1)S(1)}, bf16[416,128]{1,0:T(8,128)(2,1)}, u32[]{:S(2)}) copy-start(bf16[416,128]{1,0:T(8,128)(2,1)} %get-tuple-element.5) | copy-start | bytes 319492

commit v4 on v3

--- a/solution.py
+++ b/solution.py
@@ -9,7 +9,9 @@
 HEAD = 64
 PADDED = 896
 CHUNKS = 4
-COPIES = 96
+COPIES = 84
+Z_FIRST = 2
+MADE = (0, 2, 1, 3)
 norm_eps = 1e-05
 MESH = pl.DeviceIdType.MESH
 BF = jnp.bfloat16
@@ -22,7 +24,7 @@
     alen, tlen, frames, kernel, text, gain, cot, w_hbm,
     hidden_out, grad_out, frames_out,
     gains, w, xh, xt, taps, frm, pa, sta, rxa, stz, rza, stat_out, stat_in, gacc, tacc, sqs, gst, tst, grx,
-    totals, gall, coefs, bst, brx, xst, xown, xrx, zst, zrx,
+    totals, gall, coefs, bst, brx, xst, xown, xrx, zst, zrx, zfirst,
     send_sems, recv_sems, local_sem,
 ):
     batch, hid, y = (lax.axis_index(a) for a in ("batch", "hidden", "width"))
@@ -400,6 +402,12 @@
             xst[:, lanes] = out.astype(BF)
 
         tiles(span // 512, tile)
+        if j == Z_FIRST:
+            x_copies[j] = group(
+                zfirst,
+                [(xst.at[:, piece(j, zmod(k))], zfirst.at[k - 1], z_peers[k - 1]) for k in (4, 3, 5, 2, 6, 1, 7)],
+            )
+            return
         x_copies[j] = group(
             xrx.at[:, :, columns(j)],
             [
@@ -408,17 +416,32 @@
             ],
         )
 
-    to_sibling(0)
-    for j in range(CHUNKS):
-        if j + 1 < CHUNKS:
-            to_sibling(j + 1)
-        to_x(j)
+    to_sibling(MADE[0])
+    for i in range(CHUNKS):
+        if i + 1 < CHUNKS:
+            to_sibling(MADE[i + 1])
+        to_x(MADE[i])
     arrive(cross_copy)
     tail_fwd = send(xt.at[theirs], xt.at[theirs], sibling)
     mine32 = rows(x * 32, 32)
 
     def x_sum(j):
         arrive(x_copies[j])
+        if j == Z_FIRST:
+            lanes = piece(j, z)
+            out = xown[:, lanes]
+            for k in range(7):
+                out = out + zfirst[k].astype(F32)
+            xown[:, lanes] = out
+            xst[:, lanes] = out.astype(BF)
+            first_part = pl.ds(j * span, part)
+            return group(
+                xrx.at[:, :, first_part],
+                [
+                    (xst.at[rows(xmod(k) * 32, 32), lanes], xrx.at[k - 1, :, first_part], x_peers[k - 1])
+                    for k in (2, 1, 3)
+                ],
+            )
         out = xown[mine32, columns(j)]
         for k in range(3):
             out = out + xrx[k, :, columns(j)].astype(F32)
@@ -430,8 +453,12 @@
         arrive(copies)
         lanes = piece(j, z)
         total = xown[mine32, lanes]
-        for k in range(7):
-            total = total + zrx[k, :, pl.ds(j * part, part)].astype(F32)
+        if j == Z_FIRST:
+            for k in range(3):
+                total = total + xrx[k, :, pl.ds(j * span, part)].astype(F32)
+        else:
+            for k in range(7):
+                total = total + zrx[k, :, pl.ds(j * part, part)].astype(F32)
         grad_out[place, lanes] = total.astype(BF)
 
     tail_y = []
@@ -503,6 +530,7 @@
         ((3, 32, width_here), BF),
         ((32, width_here), SUMS_B),
         ((7, 32, width_here // 8), SUMS_B),
+        ((7, 128, width_here // (8 * CHUNKS)), BF),
     ]
     hidden, grad, frames_t = pl.pallas_call(
         fused_kernel,

time: 111 us -> 112 us (level)
  no operation moved by 1% of the time
where the time goes in v4:
time: 112 us; the launch traced here: 111 us
  Pallas kernels  109 us (97%)
  between operations  1.94 us (2%)
    pallas_call x1, Pallas kernels, on_device(): pl.pallas_call(fused_kernel, out_shape=(jax.ShapeDtypeStruct((units // 2,...  104 us
    pallas_call x1, Pallas kernels, on_device(): pl.pallas_call(weight_kernel, grid=(width_here // tile,), out_shape=jax.S...  5 us

profile of v4, /device:TPU:1, one launch (start us, length us, event | category | flops | bytes accessed | tf_op | source)
XLA Modules:
  0.0 111.4 jit_solution(15705933959970752970)
XLA Ops:
  1.9 103.9 %shard_map.95 = (bf16[416,128]{1,0:T(8,128)(2,1)}, bf16[256,4096]{1,0:T(8,128)(2,1)}, bf16[320,256]{1,0:T(8,128)(2,1)}) custom-call(s32[1]{0:T(128)S(6)} %copy.11.alen, s32[1]{0:T(128)S(6)} %copy.12.tlen, bf16[80,512]{1,0:T(8,128)(2,1)} %bitcast.12, bf16[4,80,4096]{2,1,0:T(8,128)(2,1)} %kernel.1, bf16[128,4096]{1,0:T(8,128)(2,1)} %text.1, ...), custom_call_target="tpu_custom_call" | custom-call | tf_op jit(solution)/shard_map/pallas_call | solution.py:535
  105.8 0.0 copy-start
  105.8 5.0 %shard_map.96 = f32[4,80,4096]{2,1,0:T(8,128)} custom-call(bf16[320,256]{1,0:T(8,128)(2,1)} %get-tuple-element.6.frames_t, bf16[256,4096]{1,0:T(8,128)(2,1)} %get-tuple-element.7.grad), custom_call_target="tpu_custom_call" | custom-call | tf_op jit(solution)/shard_map/pallas_call | solution.py:555
  110.8 0.0 copy-done
  110.8 0.6 copy.13
Async XLA Ops:
  105.8 5.0 %copy-start = (bf16[416,128]{1,0:T(8,128)(2,1)S(1)}, bf16[416,128]{1,0:T(8,128)(2,1)}, u32[]{:S(2)}) copy-start(bf16[416,128]{1,0:T(8,128)(2,1)} %get-tuple-element.5) | copy-start | bytes 319492

commit v5 on v3

--- a/solution.py
+++ b/solution.py
@@ -9,13 +9,13 @@
 HEAD = 64
 PADDED = 896
 CHUNKS = 4
-COPIES = 96
+COPIES = 84
 norm_eps = 1e-05
 MESH = pl.DeviceIdType.MESH
 BF = jnp.bfloat16
 F32 = jnp.float32
 SUMS_A = BF
-SUMS_B = F32
+SUMS_B = BF
 
 
 def fused_kernel(
@@ -385,7 +385,7 @@
     def to_sibling(j):
         def tile(i):
             lanes = lanes_of(j * (span // 512) + i, 512)
-            bst[:, lanes] = share((1 - c) * 128, lanes).astype(BF)
+            bst[:, lanes] = share((1 - c) * 128, lanes)
 
         tiles(span // 512, tile)
         sib_copies[j] = send(bst.at[:, columns(j)], brx.at[:, columns(j)], sibling)
@@ -395,7 +395,7 @@
 
         def tile(i):
             lanes = lanes_of(j * (span // 512) + i, 512)
-            out = share(c * 128, lanes) + brx[:, lanes].astype(F32)
+            out = share(c * 128, lanes) + brx[:, lanes]
             xown[:, lanes] = out
             xst[:, lanes] = out.astype(BF)
 
@@ -496,8 +496,8 @@
         ((128, PADDED), F32),
         ((256, PADDED), BF),
         ((256, 128), F32),
-        ((128, width_here), BF),
-        ((128, width_here), BF),
+        ((128, width_here), F32),
+        ((128, width_here), F32),
         ((128, width_here), BF),
         ((128, width_here), F32),
         ((3, 32, width_here), BF),

time: 111 us -> 108 us (0.973)
  Pallas kernels: 108 us -> 105 us
    pallas_call x1, Pallas kernels: 103 us -> 100 us  [on_device(): pl.pallas_call(fused_kernel, out_shape=(jax.ShapeDtypeStruct((units // 2,...]
where the time goes in v5:
time: 108 us
  Pallas kernels  105 us (97%)
  between operations  1.94 us (2%)
    pallas_call x1, Pallas kernels, on_device(): pl.pallas_call(fused_kernel, out_shape=(jax.ShapeDtypeStruct((units // 2,...  100 us
    pallas_call x1, Pallas kernels, on_device(): pl.pallas_call(weight_kernel, grid=(width_here // tile,), out_shape=jax.S...  5 us

profile of v5, /device:TPU:1, one launch (start us, length us, event | category | flops | bytes accessed | tf_op | source)
XLA Modules:
  0.0 107.7 jit_solution(5553709749629443699)
XLA Ops:
  1.9 100.1 %shard_map.95 = (bf16[416,128]{1,0:T(8,128)(2,1)}, bf16[256,4096]{1,0:T(8,128)(2,1)}, bf16[320,256]{1,0:T(8,128)(2,1)}) custom-call(s32[1]{0:T(128)S(6)} %copy.11.alen, s32[1]{0:T(128)S(6)} %copy.12.tlen, bf16[80,512]{1,0:T(8,128)(2,1)} %bitcast.12, bf16[4,80,4096]{2,1,0:T(8,128)(2,1)} %kernel.1, bf16[128,4096]{1,0:T(8,128)(2,1)} %text.1, ...), custom_call_target="tpu_custom_call" | custom-call | tf_op jit(solution)/shard_map/pallas_call | solution.py:507
  102.1 0.0 copy-start
  102.1 5.0 %shard_map.96 = f32[4,80,4096]{2,1,0:T(8,128)} custom-call(bf16[320,256]{1,0:T(8,128)(2,1)} %get-tuple-element.6.frames_t, bf16[256,4096]{1,0:T(8,128)(2,1)} %get-tuple-element.7.grad), custom_call_target="tpu_custom_call" | custom-call | tf_op jit(solution)/shard_map/pallas_call | solution.py:527
  107.1 0.0 copy-done
  107.1 0.6 copy.13
Async XLA Ops:
  102.1 5.0 %copy-start = (bf16[416,128]{1,0:T(8,128)(2,1)S(1)}, bf16[416,128]{1,0:T(8,128)(2,1)}, u32[]{:S(2)}) copy-start(bf16[416,128]{1,0:T(8,128)(2,1)} %get-tuple-element.5) | copy-start | bytes 319492
